TPU v7x, 32 devices: a whole 2x2x4 slice. The times are simulated.
32 devices in a mesh: wide: 8 (over z, x), narrow: 4 (over y, core).
Axes of the slice: x: 2, y: 2, z: 4, core: 2. Of those that a mesh axis runs over, the one named last changes fastest.
Arguments:
- tile_data: bfloat16 [10240, 128, 128], P(('wide', 'narrow')), may hold values from -0.119628906 to 0.119628906
- tile_user: int32 [10240], P(('wide', 'narrow')), may hold values from 0 to 15
- tile_item: int32 [10240], P(('wide', 'narrow')), may hold values from 0 to 7
- tile_word: int32 [10240], P(('wide', 'narrow')), may hold values from 0 to 4095
- tile_month: int32 [10240], P(('wide', 'narrow')), may hold values from 0 to 999
- tile_live: int32 [32], P(('wide', 'narrow')), may hold values from 160 to 320, as said below
- user_need: int32 [32, 16], P(('wide', 'narrow')), may hold values from 0 to 127, as said below
- item_need: int32 [32, 8], P(('wide', 'narrow')), may hold values from 0 to 127, as said below
- user_slot: int32 [128], replicated, may hold values from 0 to 127, as said below
- item_slot: int32 [128], replicated, may hold values from 0 to 127, as said below
- user_factor: bfloat16 [16384, 128], P('wide'), may hold values from -6 to 6
- word_factor: bfloat16 [4096, 128], replicated, may hold values from -6 to 6
- month_factor: bfloat16 [1000, 128], replicated, may hold values from -6 to 6
Outputs:
- item_rows: float32 [16384, 128], P(('wide', 'narrow'))
Inputs may be any that keep to these rules, and one draw needn't show every extreme that they name: user_slot is a permutation; the owner of user block b is user_slot[b] // 16. item_slot is a permutation; the owner of item block b is item_slot[b] // 16. `user_need`: entries k * 2 to k * 2 + 1 of each row are distinct user blocks whose owner is k. `item_need`: entry k of each row is an item block whose owner is k. `tile_live`: some device has all its slots live.
All inputs are finite; a program needn't handle non-finite values.
Results may differ from a plain program's by a relative error of at most 0.0029.
Values may be sent and summed in bfloat16 or wider, within the bound.
No kernel may reach another device: no remote copies, remote signals or barrier semaphores. Data moves between devices by JAX's collectives and lax.ppermute only.
A program may use at most 128 MiB of HBM per device.

v0:
```python
import functools

import jax
import jax.numpy as jnp
from jax import lax
from jax.experimental import pallas as pl
from jax.experimental.pallas import tpu as pltpu
from jax.sharding import PartitionSpec as P

CONTRACT_MIB = 12
ANSWER_MIB = 12
RANK_MIB = 63
TURN_MIB = 12
TURN = 32
GROUP = 4
CHUNKS = 12
SMEM = pl.BlockSpec(memory_space=pltpu.SMEM)
VMEM = pl.BlockSpec(memory_space=pltpu.VMEM)
HBM = pl.BlockSpec(memory_space=pltpu.HBM)


def lanes(n):
    return -(-n // 128) * 128


def rank_kernel(slots, touched, me, live, user, item, lay, work):
    tile_count = item.shape[0]
    dump = slots - 16
    iota = lambda shape, dim: lax.broadcasted_iota(jnp.int32, shape, dim)
    as_half = lambda mask: jnp.where(mask, 1.0, 0.0).astype(jnp.bfloat16)
    chunks_of = lambda n: jnp.floor((n + (GROUP - 1)) * (1.0 / GROUP))
    across = (((1,), (1,)), ((), ()))
    lane = iota((1, tile_count), 1)
    alive = lane < live[...].reshape(1, 1)
    one = jnp.where((iota((touched, tile_count), 0) == item[...].reshape(1, tile_count)) & alive, 1.0, 0.0)
    half = one.astype(jnp.bfloat16)
    before = as_half(iota((tile_count, tile_count), 0) < iota((tile_count, tile_count), 1))
    earlier = jnp.dot(half, before, preferred_element_type=jnp.float32)
    chunks = chunks_of(jnp.sum(one, axis=1, keepdims=True))
    small = (touched, touched)
    offset = GROUP * jnp.dot(
        as_half(iota(small, 1) < iota(small, 0)),
        jnp.broadcast_to(chunks, (touched, 128)).astype(jnp.bfloat16),
        preferred_element_type=jnp.float32,
    )[:, :1]
    here = jnp.sum(one * (earlier + offset), axis=0, keepdims=True).astype(jnp.int32)
    place = jnp.where(alive, here, dump + lax.rem(lane, 16))
    count_row = lax.dot_general(
        jnp.ones((8, tile_count), jnp.bfloat16), half, across, preferred_element_type=jnp.float32
    )
    offset_row = GROUP * jnp.dot(
        chunks_of(count_row).astype(jnp.bfloat16),
        as_half(iota(small, 0) < iota(small, 1)),
        preferred_element_type=jnp.float32,
    )
    at = lanes(tile_count)
    lay[:, 0:tile_count] = place
    lay[:, at : at + touched] = count_row[0:1].astype(jnp.int32)
    at += lanes(touched)
    lay[:, at : at + touched] = offset_row[0:1].astype(jnp.int32)
    user_row = jnp.broadcast_to(user[...].reshape(1, tile_count), (8, tile_count))
    users = lax.dot_general(
        user_row.astype(jnp.float32).astype(jnp.bfloat16),
        as_half(iota((slots, tile_count), 0) == place),
        across,
        preferred_element_type=jnp.float32,
    )
    end = (offset + GROUP * chunks).astype(jnp.int32)
    used = jnp.sum(GROUP * chunks, axis=0, keepdims=True).astype(jnp.int32)
    width = lanes(slots // GROUP)
    passed = jnp.where(GROUP * iota((touched, width), 1) >= end, 1, 0)
    work[:, 0:slots] = users[0:1].astype(jnp.int32)
    at = lanes(slots)
    work[:, at : at + width] = jnp.minimum(jnp.sum(passed, axis=0, keepdims=True), touched - 1)
    at += width
    work[:, at : at + 128] = jnp.broadcast_to(used, (1, 128))
    work[:, at + 128 : at + 256] = jnp.broadcast_to(me[0], (1, 128))


def slots_for(tile_count, touched):
    per_step = GROUP * CHUNKS
    return -(-(tile_count + touched * (GROUP - 1)) // per_step) * per_step + per_step + 16


def rank(me, live, user, item, touched):
    tile_count = user.shape[0]
    slots = slots_for(tile_count, touched)
    row = lambda n: jax.ShapeDtypeStruct((1, n), jnp.int32)
    return pl.pallas_call(
        functools.partial(rank_kernel, slots, touched),
        out_shape=(
            row(lanes(tile_count) + 2 * lanes(touched)),
            row(lanes(slots) + lanes(slots // GROUP) + 256),
        ),
        in_specs=[SMEM, VMEM, VMEM, VMEM],
        out_specs=(VMEM, VMEM),
        compiler_params=pltpu.CompilerParams(vmem_limit_bytes=RANK_MIB << 20),
        cost_estimate=pl.CostEstimate(flops=1 << 33, bytes_accessed=1 << 25, transcendentals=0),
        name="rank",
    )(me, live, user, item)


def turn_kernel(touched, lay, word, month, tiles, words, months, turned, scale, word_rows, month_rows):
    tile_count = tiles.shape[0]
    dump = turned.shape[0] - 16
    counts = lanes(tile_count)
    offsets = counts + lanes(touched)
    word_rows[...] = words[...].astype(jnp.float32)
    month_rows[...] = months[...].astype(jnp.float32)
    nothing = jnp.zeros(turned.shape[1:], turned.dtype)
    no_scale = jnp.zeros((1, scale.shape[1]), scale.dtype)

    def clear(p):
        turned[p] = nothing
        scale[pl.ds(p, 1), :] = no_scale

    def clear_item(q, _):
        end = lay[0, offsets + q] + lay[0, counts + q]
        for j in range(GROUP - 1):
            clear(jnp.where(lax.rem(end + j, GROUP) > lax.rem(end + GROUP - 1, GROUP), end + j, dump + j))
        return lax.div(end + GROUP - 1, GROUP) * GROUP

    used = lax.fori_loop(0, touched, clear_item, 0)

    def clear_rest(n, _):
        clear(used + n)
        return 0

    lax.fori_loop(0, GROUP * (CHUNKS - 1), clear_rest, 0, unroll=4)

    def put(c, _):
        for n in range(TURN):
            t = c * TURN + n
            p = lay[0, t]
            turned[p] = tiles[t].T
            scale[pl.ds(p, 1), :] = (
                word_rows[pl.ds(word[t], 1), :] * month_rows[pl.ds(month[t], 1), :]
            )
        return 0

    lax.fori_loop(0, tile_count // TURN, put, 0)


def turn(lay, word, month, tiles, words, months, slots, touched):
    side = tiles.shape[1]
    width = words.shape[1]
    return pl.pallas_call(
        functools.partial(turn_kernel, touched),
        out_shape=(
            jax.ShapeDtypeStruct((slots, side, side), tiles.dtype),
            jax.ShapeDtypeStruct((slots, width), jnp.float32),
        ),
        in_specs=[SMEM, SMEM, SMEM, VMEM, VMEM, VMEM],
        out_specs=(VMEM, VMEM),
        scratch_shapes=[
            pltpu.VMEM(words.shape, jnp.float32),
            pltpu.VMEM(months.shape, jnp.float32),
        ],
        compiler_params=pltpu.CompilerParams(vmem_limit_bytes=TURN_MIB << 20),
        cost_estimate=pl.CostEstimate(
            flops=1 << 30, bytes_accessed=4 * tiles.size, transcendentals=0
        ),
        name="turn",
    )(lay, word, month, tiles, words, months)


def ask_kernel(user_need, item_need, need):
    wide, _, both = need.shape
    users = user_need.shape[1]
    need[:, :, 0:users] = jnp.broadcast_to(user_need[...][None], (wide, 1, users))
    need[:, :, users:both] = jnp.broadcast_to(item_need[...][None], (wide, 1, both - users))


def ask(user_need, item_need, wide):
    both = user_need.shape[1] + item_need.shape[1]
    return pl.pallas_call(
        ask_kernel,
        out_shape=jax.ShapeDtypeStruct((wide, 1, both), jnp.int32),
        in_specs=[VMEM, VMEM],
        out_specs=VMEM,
        compiler_params=pltpu.CompilerParams(vmem_limit_bytes=63 << 20),
        name="ask",
    )(user_need, item_need)


def answer_kernel(owned, per, me, heard, slot, blocks, *outs):
    for d, out in enumerate(outs):
        k = me[0] ^ d
        for j in range(per):
            out[j] = blocks[lax.rem(slot[heard[k, 0, me[0] * per + j]], owned)]


def answer(me, heard, slot, blocks, per):
    owned, side, width = blocks.shape
    wide = heard.shape[0]
    return pl.pallas_call(
        functools.partial(answer_kernel, owned, per),
        out_shape=(jax.ShapeDtypeStruct((per, side, width), blocks.dtype),) * wide,
        in_specs=[SMEM, SMEM, SMEM, VMEM],
        out_specs=(VMEM,) * wide,
        compiler_params=pltpu.CompilerParams(vmem_limit_bytes=ANSWER_MIB << 20),
        cost_estimate=pl.CostEstimate(flops=1 << 33, bytes_accessed=1 << 25, transcendentals=0),
        name="answer",
    )(me, heard, slot, blocks)


def contract_kernel(work, scale, turned, *refs):
    fetched, (out, wide_blocks, total) = refs[:-3], refs[-3:]
    per = fetched[0].shape[0]
    per_step = GROUP * CHUNKS
    items = lanes(scale.shape[0])
    used = items + lanes(scale.shape[0] // GROUP)
    me = work[0, used + 128]
    for d, blocks in enumerate(fetched):
        for j in range(per):
            wide_blocks[(me ^ d) * per + j] = blocks[j].astype(jnp.float32)
    total[...] = jnp.zeros_like(total)

    def step(i, _):
        first = i * per_step
        for c in range(CHUNKS):
            left, right = [], []
            for g in range(GROUP):
                p = first + c * GROUP + g
                left.append(turned[p])
                right.append((wide_blocks[work[0, p]] * scale[pl.ds(p, 1), :]).astype(jnp.bfloat16))
            part = jnp.dot(
                jnp.concatenate(left, 1),
                jnp.concatenate(right, 0),
                preferred_element_type=jnp.float32,
            )
            q = work[0, items + i * CHUNKS + c]
            total[q] = total[q] + part
        return 0

    steps = (work[0, used] + per_step - 1) // per_step
    lax.fori_loop(0, steps, step, 0)
    out[...] = total[...].astype(out.dtype)


def contract(work, scale, turned, fetched, touched):
    per, side, width = fetched[0].shape
    return pl.pallas_call(
        contract_kernel,
        out_shape=jax.ShapeDtypeStruct((touched, side, width), jnp.bfloat16),
        in_specs=[SMEM, VMEM, VMEM] + [VMEM] * len(fetched),
        out_specs=VMEM,
        scratch_shapes=[
            pltpu.VMEM((len(fetched) * per, side, width), jnp.float32),
            pltpu.VMEM((touched, side, width), jnp.float32),
        ],
        compiler_params=pltpu.CompilerParams(vmem_limit_bytes=CONTRACT_MIB << 20),
        cost_estimate=pl.CostEstimate(
            flops=2 * turned.size * width, bytes_accessed=turned.size, transcendentals=0
        ),
        name="contract",
    )(work, scale, turned, *fetched)


def merge_kernel(items_owned, per, owner, me, heard, slot, parts, mine, *rest):
    sends, total = rest[:-1], rest[-1]
    share = mine.shape[0]
    total[...] = jnp.zeros_like(total)

    base = heard.shape[2] - per * heard.shape[0] + per * owner[0]

    def add(k, _):
        for n in range(per):
            j = lax.rem(slot[heard[k, 0, base + n]], items_owned)
            total[j] = total[j] + parts[k * per + n].astype(jnp.float32)
        return 0

    lax.fori_loop(0, heard.shape[0], add, 0)
    for d in range(items_owned // share):
        first = (me[0] ^ d) * share
        for j in range(share):
            if d == 0:
                mine[j] = total[first + j]
            else:
                sends[d - 1][j] = total[first + j].astype(jnp.bfloat16)


def merge(owner, me, heard, slot, parts, items_owned, members, per):
    side, width = parts.shape[1:]
    share = items_owned // members
    piece = lambda kind: jax.ShapeDtypeStruct((share, side, width), kind)
    return pl.pallas_call(
        functools.partial(merge_kernel, items_owned, per),
        out_shape=(piece(jnp.float32),) + (piece(jnp.bfloat16),) * (members - 1),
        in_specs=[SMEM, SMEM, SMEM, SMEM, VMEM],
        out_specs=(VMEM,) * members,
        scratch_shapes=[pltpu.VMEM((items_owned, side, width), jnp.float32)],
        compiler_params=pltpu.CompilerParams(vmem_limit_bytes=12 << 20),
        name="merge",
    )(owner, me, heard, slot, parts)


def body(
    tile_data,
    tile_user,
    tile_item,
    tile_word,
    tile_month,
    tile_live,
    user_need,
    item_need,
    user_slot,
    item_slot,
    user_factor,
    word_factor,
    month_factor,
):
    wide = lax.axis_size("wide")
    members = lax.axis_size("narrow")
    side = tile_data.shape[1]
    width = user_factor.shape[1]
    touched = item_need.shape[1]
    items_owned = item_slot.shape[0] // wide
    per_user = user_need.shape[1] // wide
    need = ask(user_need, item_need, wide)
    heard = lax.all_to_all(need, "wide", split_axis=0, concat_axis=0, tiled=True)
    me_wide = lax.axis_index("wide").reshape(1)
    lay, work = rank(me_wide, tile_live, tile_user, tile_item, touched)
    replies = answer(me_wide, heard, user_slot, user_factor.reshape(-1, side, width), per_user)
    fetched = list(replies)
    for d in reversed(range(1, wide)):
        fetched[d] = lax.ppermute(replies[d], "wide", [(k, k ^ d) for k in range(wide)])
    turned, scale = turn(
        lay,
        tile_word,
        tile_month,
        tile_data,
        word_factor,
        month_factor,
        slots_for(tile_data.shape[0], touched),
        touched,
    )
    partial = contract(work, scale, turned, fetched, touched)
    arrived = lax.all_to_all(
        partial.reshape(wide, -1, side, width), "wide", split_axis=0, concat_axis=0, tiled=True
    ).reshape(-1, side, width)
    me = lax.axis_index("narrow").reshape(1)
    pieces = merge(me_wide, me, heard, item_slot, arrived, items_owned, members, touched // wide)
    rows = pieces[0]
    for d in range(1, members):
        got = lax.ppermute(pieces[d], "narrow", [(n, n ^ d) for n in range(members)])
        rows = rows + got.astype(jnp.float32)
    return rows.reshape(-1, width)


def solution(mesh):
    return jax.shard_map(
        body,
        mesh=mesh,
        in_specs=(
            P(("wide", "narrow"), None, None),
            P(("wide", "narrow")),
            P(("wide", "narrow")),
            P(("wide", "narrow")),
            P(("wide", "narrow")),
            P(("wide", "narrow")),
            P(("wide", "narrow"), None),
            P(("wide", "narrow"), None),
            P(),
            P(),
            P("wide", None),
            P(),
            P(),
        ),
        out_specs=P(("wide", "narrow"), None),
        check_vma=False,
    )
```

profile of v0, /device:TPU:0, one launch (start us, length us, event | category | flops | bytes accessed | tf_op | source)
XLA Modules:
  0.0 68.5 jit_solution(4568515964293895342)
XLA Ops:
  0.0 1.3 %ask.1 = s32[8,1,24]{2,1,0:T(1,128)} custom-call(s32[1,16]{1,0:T(1,128)} %user_need.1, s32[1,8]{1,0:T(1,128)} %item_need.1), custom_call_target="tpu_custom_call" | custom-call | tf_op jit(solution)/shard_map/ask/pallas_call | solution.py:176
  1.3 7.3 %all-to-all-start = ((s32[8,1,24]{2,1,0:T(1,128)}), s32[8,1,24]{2,1,0:T(1,128)S(1)}, u32[]{:S(2)}, u32[]{:S(2)}) async-start(s32[8,1,24]{2,1,0:T(1,128)} %ask.1), calls=%async_computation | async-start | bytes 8192 | tf_op jit(solution)/shard_map/all_to_all | solution.py:321
  9.3 5.8 %all-to-all-done.heard = s32[8,1,24]{2,1,0:T(1,128)S(1)} async-done(((s32[8,1,24]{2,1,0:T(1,128)}), s32[8,1,24]{2,1,0:T(1,128)S(1)}, u32[]{:S(2)}, u32[]{:S(2)}) %all-to-all-start) | async-done | bytes 800 | tf_op jit(solution)/shard_map/all_to_all | solution.py:321
  15.0 0.0 copy-start.8
  15.0 1.0 %copy-done.8 = bf16[2048,128]{1,0:T(8,128)(2,1)S(1)} copy-done((bf16[2048,128]{1,0:T(8,128)(2,1)S(1)}, bf16[2048,128]{1,0:T(8,128)(2,1)}, u32[]{:S(2)}) %copy-start.8) | copy-done | bytes 524312
  16.1 0.0 copy-start.9
  16.1 0.7 copy-done.9
  16.7 0.7 answer.1
  17.4 0.6 collective-permute-start
  18.0 0.0 copy-start.2
  18.0 0.0 copy-start.5
  18.0 0.6 collective-permute-start.1
  18.6 1.8 %rank.1 = (s32[1,640]{1,0:T(1,128)}, s32[1,896]{1,0:T(1,128)}) custom-call(s32[1]{0:T(128)} %bitcast.me.owner, s32[1]{0:T(128)S(6)} %copy.15.live, s32[320]{0:T(512)} %user.1, s32[320]{0:T(512)} %item.1), custom_call_target="tpu_custom_call" | custom-call | flops 8589934592 | bytes 33554432 | tf_op jit(solution)/shard_map/rank/pallas_call | solution.py:89
  20.5 0.0 copy-start.7
  20.5 2.4 %collective-permute-start.2 = (bf16[2,128,128]{2,1,0:T(8,128)(2,1)S(1)}, bf16[2,128,128]{2,1,0:T(8,128)(2,1)S(1)}, u32[]{:S(2)}, u32[]{:S(2)}) collective-permute-start(bf16[2,128,128]{2,1,0:T(8,128)(2,1)S(1)} %get-tuple-element.28), channel_id=1, source_target_pairs={{0,12},{4,8},{8,4},{12,0},{16,28},{20,24},{24,20},{28,16},{1,13},{... | collective-permute-start | bytes 196616 | tf_op jit(solution)/shard_map/ppermute | solution.py:327
  22.8 0.6 collective-permute-start.3
  23.4 2.4 %collective-permute-start.4 = (bf16[2,128,128]{2,1,0:T(8,128)(2,1)S(1)}, bf16[2,128,128]{2,1,0:T(8,128)(2,1)S(1)}, u32[]{:S(2)}, u32[]{:S(2)}) collective-permute-start(bf16[2,128,128]{2,1,0:T(8,128)(2,1)S(1)} %get-tuple-element.30), channel_id=1, source_target_pairs={{0,20},{4,16},{8,28},{12,24},{16,4},{20,0},{24,12},{28,8},{1,21},{... | collective-permute-start | bytes 196616 | tf_op jit(solution)/shard_map/ppermute | solution.py:327
  25.7 0.0 collective-permute-done.refs_1_
  25.7 0.6 collective-permute-start.5
  26.3 0.0 collective-permute-done.1.refs_2_
  26.3 4.1 %collective-permute-start.6 = (bf16[2,128,128]{2,1,0:T(8,128)(2,1)S(1)}, bf16[2,128,128]{2,1,0:T(8,128)(2,1)S(1)}, u32[]{:S(2)}, u32[]{:S(2)}) collective-permute-start(bf16[2,128,128]{2,1,0:T(8,128)(2,1)S(1)} %get-tuple-element.32), channel_id=1, source_target_pairs={{0,28},{4,24},{8,20},{12,16},{16,12},{20,8},{24,4},{28,0},{1,29},{... | collective-permute-start | bytes 196616 | tf_op jit(solution)/shard_map/ppermute | solution.py:327
  30.5 0.0 copy-done.2
  30.5 0.0 copy-done.5
  30.5 0.0 copy-done.6
  30.5 0.0 copy-start
  30.5 4.0 %copy-done = bf16[320,128,128]{2,1,0:T(8,128)(2,1)S(1)} copy-done((bf16[320,128,128]{2,1,0:T(8,128)(2,1)S(1)}, bf16[320,128,128]{2,1,0:T(8,128)(2,1)}, u32[]{:S(2)}) %copy-start) | copy-done | bytes 10485784
  34.5 1.2 %copy-done.1 = bf16[4096,128]{1,0:T(8,128)(2,1)S(1)} copy-done((bf16[4096,128]{1,0:T(8,128)(2,1)S(1)}, bf16[4096,128]{1,0:T(8,128)(2,1)}, u32[]{:S(2)}) %copy-start.1) | copy-done | bytes 1048600
  35.7 0.7 copy-done.4
  36.4 4.5 %turn.1 = (bf16[448,128,128]{2,1,0:T(8,128)(2,1)S(1)}, f32[448,128]{1,0:T(8,128)S(1)}) custom-call(s32[1,640]{1,0:T(1,128)S(1)} %copy-done.4, s32[320]{0:T(512)S(1)} %copy-done.5, s32[320]{0:T(512)S(1)} %copy-done.6, bf16[320,128,128]{2,1,0:T(8,128)(2,1)S(1)} %copy-done, bf16[4096,128]{1,0:T(8,128)(2,1)S(1)} %copy-done.1, bf16[1000,128]{1,0:T(8,128)(2,1)S(1)} %copy-done.2), custom_call_target="tpu_custom_call" | custom-call | flops 1073741824 | bytes 20971520 | tf_op jit(solution)/shard_map/turn/pallas_call | solution.py:147
  40.9 0.0 collective-permute-done.2.refs_3_
  40.9 0.0 collective-permute-done.3.refs_4_
  40.9 0.0 collective-permute-done.4.refs_5_
  40.9 0.0 collective-permute-done.5.refs_6_
  40.9 0.0 collective-permute-done.6.refs_7_
  41.0 0.0 copy-start.3
  41.0 0.7 copy-done.3
  41.6 5.4 %contract.1 = bf16[8,128,128]{2,1,0:T(8,128)(2,1)} custom-call(s32[1,896]{1,0:T(1,128)S(1)} %copy-done.3, f32[448,128]{1,0:T(8,128)S(1)} %get-tuple-element.23.scale, bf16[448,128,128]{2,1,0:T(8,128)(2,1)S(1)} %get-tuple-element.24.turned, bf16[2,128,128]{2,1,0:T(8,128)(2,1)S(1)} %get-tuple-element.25.refs_0_, ...), custom_call_target="tpu_custom_call" | custom-call | flops 1879048192 | bytes 7340032 | tf_op jit(solution)/shard_map/contract/pallas_call | solution.py:243
  47.1 3.4 %all-to-all-start.1 = ((bf16[8,1,128,128]{3,2,1,0:T(8,128)(2,1)}), bf16[8,1,128,128]{3,2,1,0:T(8,128)(2,1)S(1)}, u32[]{:S(2)}, u32[]{:S(2)}) async-start(bf16[8,1,128,128]{3,2,1,0:T(8,128)(2,1)} %bitcast.4), calls=%async_computation.1 | async-start | bytes 524288 | tf_op jit(solution)/shard_map/all_to_all | solution.py:339
  50.5 8.2 %all-to-all-done.1 = bf16[8,1,128,128]{3,2,1,0:T(8,128)(2,1)S(1)} async-done(((bf16[8,1,128,128]{3,2,1,0:T(8,128)(2,1)}), bf16[8,1,128,128]{3,2,1,0:T(8,128)(2,1)S(1)}, u32[]{:S(2)}, u32[]{:S(2)}) %all-to-all-start.1) | async-done | bytes 262176 | tf_op jit(solution)/shard_map/all_to_all | solution.py:339
  58.7 0.0 copy-done.7
  58.7 0.9 %merge.1 = (f32[4,128,128]{2,1,0:T(8,128)S(1)}, bf16[4,128,128]{2,1,0:T(8,128)(2,1)S(1)}, bf16[4,128,128]{2,1,0:T(8,128)(2,1)S(1)}, bf16[4,128,128]{2,1,0:T(8,128)(2,1)S(1)}) custom-call(s32[1]{0:T(128)} %bitcast.me.owner, s32[1]{0:T(128)} %bitcast.1.me, s32[8,1,24]{2,1,0:T(1,128)S(1)} %all-to-all-done.heard, s32[128]{0:T(128)S(1)} %copy-done.7, ...), custom_call_target="tpu_custom_call" | custom-call | tf_op jit(solution)/shard_map/merge/pallas_call | solution.py:287
  59.5 0.1 collective-permute-start.7
  59.6 0.4 collective-permute-start.8
  60.1 1.4 %collective-permute-start.9 = (bf16[4,128,128]{2,1,0:T(8,128)(2,1)S(1)}, bf16[4,128,128]{2,1,0:T(8,128)(2,1)S(1)}, u32[]{:S(2)}, u32[]{:S(2)}) collective-permute-start(bf16[4,128,128]{2,1,0:T(8,128)(2,1)S(1)} %get-tuple-element.36), channel_id=1, source_target_pairs={{0,3},{1,2},{2,1},{3,0},{4,7},{5,6},{6,5},{7,4},{8,11},{9,10},{10,... | collective-permute-start | bytes 393224 | tf_op jit(solution)/shard_map/ppermute | solution.py:346
  61.5 0.0 collective-permute-done.7
  61.5 4.6 %collective-permute-done.8 = bf16[4,128,128]{2,1,0:T(8,128)(2,1)S(1)} collective-permute-done((bf16[4,128,128]{2,1,0:T(8,128)(2,1)S(1)}, bf16[4,128,128]{2,1,0:T(8,128)(2,1)S(1)}, u32[]{:S(2)}, u32[]{:S(2)}) %collective-permute-start.8) | collective-permute-done | bytes 131104 | tf_op jit(solution)/shard_map/ppermute | solution.py:346
  66.1 1.7 %collective-permute-done.9 = bf16[4,128,128]{2,1,0:T(8,128)(2,1)S(1)} collective-permute-done((bf16[4,128,128]{2,1,0:T(8,128)(2,1)S(1)}, bf16[4,128,128]{2,1,0:T(8,128)(2,1)S(1)}, u32[]{:S(2)}, u32[]{:S(2)}) %collective-permute-start.9) | collective-permute-done | bytes 131104 | tf_op jit(solution)/shard_map/ppermute | solution.py:346
  67.8 0.8 %convert_add_fusion = f32[4,128,128]{2,1,0:T(8,128)} fusion(bf16[4,128,128]{2,1,0:T(8,128)(2,1)S(1)} %collective-permute-done.9, bf16[4,128,128]{2,1,0:T(8,128)(2,1)S(1)} %collective-permute-done.8, f32[4,128,128]{2,1,0:T(8,128)S(1)} %get-tuple-element.33, bf16[4,128,128]{2,1,0:T(8,128)(2,1)S(1)} %collective-permute-done.7), kind=kLoop, calls=%fused_computation | loop fusion | flops 393216 | bytes 917504 | tf_op jit(solution)/shard_map/add | solution.py:347
  (3 shorter events, 0.0 us)
Async XLA Ops:
  1.3 13.7 %all-to-all-start = ((s32[8,1,24]{2,1,0:T(1,128)}), s32[8,1,24]{2,1,0:T(1,128)S(1)}, u32[]{:S(2)}, u32[]{:S(2)}) async-start(s32[8,1,24]{2,1,0:T(1,128)} %ask.1), calls=%async_computation | async-start | bytes 8192 | tf_op jit(solution)/shard_map/all_to_all | solution.py:321
  15.0 1.0 %copy-start.8 = (bf16[2048,128]{1,0:T(8,128)(2,1)S(1)}, bf16[2048,128]{1,0:T(8,128)(2,1)}, u32[]{:S(2)}) copy-start(bf16[2048,128]{1,0:T(8,128)(2,1)} %param.23) | copy-start | bytes 1572868
  16.1 0.7 copy-start.9
  17.4 8.3 %collective-permute-start = (bf16[2,128,128]{2,1,0:T(8,128)(2,1)S(1)}, bf16[2,128,128]{2,1,0:T(8,128)(2,1)S(1)}, u32[]{:S(2)}, u32[]{:S(2)}) collective-permute-start(bf16[2,128,128]{2,1,0:T(8,128)(2,1)S(1)} %get-tuple-element.26), channel_id=1, source_target_pairs={{0,4},{4,0},{8,12},{12,8},{16,20},{20,16},{24,28},{28,24},{1,5},{5... | collective-permute-start | bytes 196616 | tf_op jit(solution)/shard_map/ppermute | solution.py:327
  18.0 12.5 %copy-start.2 = (bf16[1000,128]{1,0:T(8,128)(2,1)S(1)}, bf16[1000,128]{1,0:T(8,128)(2,1)}, u32[]{:S(2)}) copy-start(bf16[1000,128]{1,0:T(8,128)(2,1)} %months.1) | copy-start | bytes 768004
  18.0 12.5 %copy-start.5 = (s32[320]{0:T(512)S(1)}, s32[320]{0:T(512)}, u32[]{:S(2)}) copy-start(s32[320]{0:T(512)} %word.1) | copy-start | bytes 3844
  18.0 12.5 %copy-start.6 = (s32[320]{0:T(512)S(1)}, s32[320]{0:T(512)}, u32[]{:S(2)}) copy-start(s32[320]{0:T(512)} %month.1) | copy-start | bytes 3844
  18.0 8.3 %collective-permute-start.1 = (bf16[2,128,128]{2,1,0:T(8,128)(2,1)S(1)}, bf16[2,128,128]{2,1,0:T(8,128)(2,1)S(1)}, u32[]{:S(2)}, u32[]{:S(2)}) collective-permute-start(bf16[2,128,128]{2,1,0:T(8,128)(2,1)S(1)} %get-tuple-element.27), channel_id=1, source_target_pairs={{0,8},{4,12},{8,0},{12,4},{16,24},{20,28},{24,16},{28,20},{1,9},{5... | collective-permute-start | bytes 196616 | tf_op jit(solution)/shard_map/ppermute | solution.py:327
  20.5 38.2 %copy-start.7 = (s32[128]{0:T(128)S(1)}, s32[128]{0:T(128)}, u32[]{:S(2)}) copy-start(s32[128]{0:T(128)} %slot.3) | copy-start | bytes 1540
  20.5 20.4 %collective-permute-start.2 = (bf16[2,128,128]{2,1,0:T(8,128)(2,1)S(1)}, bf16[2,128,128]{2,1,0:T(8,128)(2,1)S(1)}, u32[]{:S(2)}, u32[]{:S(2)}) collective-permute-start(bf16[2,128,128]{2,1,0:T(8,128)(2,1)S(1)} %get-tuple-element.28), channel_id=1, source_target_pairs={{0,12},{4,8},{8,4},{12,0},{16,28},{20,24},{24,20},{28,16},{1,13},{... | collective-permute-start | bytes 196616 | tf_op jit(solution)/shard_map/ppermute | solution.py:327
  22.8 18.1 %collective-permute-start.3 = (bf16[2,128,128]{2,1,0:T(8,128)(2,1)S(1)}, bf16[2,128,128]{2,1,0:T(8,128)(2,1)S(1)}, u32[]{:S(2)}, u32[]{:S(2)}) collective-permute-start(bf16[2,128,128]{2,1,0:T(8,128)(2,1)S(1)} %get-tuple-element.29), channel_id=1, source_target_pairs={{0,16},{4,20},{8,24},{12,28},{16,0},{20,4},{24,8},{28,12},{1,17},{... | collective-permute-start | bytes 196616 | tf_op jit(solution)/shard_map/ppermute | solution.py:327
  23.4 17.5 %collective-permute-start.4 = (bf16[2,128,128]{2,1,0:T(8,128)(2,1)S(1)}, bf16[2,128,128]{2,1,0:T(8,128)(2,1)S(1)}, u32[]{:S(2)}, u32[]{:S(2)}) collective-permute-start(bf16[2,128,128]{2,1,0:T(8,128)(2,1)S(1)} %get-tuple-element.30), channel_id=1, source_target_pairs={{0,20},{4,16},{8,28},{12,24},{16,4},{20,0},{24,12},{28,8},{1,21},{... | collective-permute-start | bytes 196616 | tf_op jit(solution)/shard_map/ppermute | solution.py:327
  25.7 15.2 %collective-permute-start.5 = (bf16[2,128,128]{2,1,0:T(8,128)(2,1)S(1)}, bf16[2,128,128]{2,1,0:T(8,128)(2,1)S(1)}, u32[]{:S(2)}, u32[]{:S(2)}) collective-permute-start(bf16[2,128,128]{2,1,0:T(8,128)(2,1)S(1)} %get-tuple-element.31), channel_id=1, source_target_pairs={{0,24},{4,28},{8,16},{12,20},{16,8},{20,12},{24,0},{28,4},{1,25},{... | collective-permute-start | bytes 196616 | tf_op jit(solution)/shard_map/ppermute | solution.py:327
  26.3 14.6 %collective-permute-start.6 = (bf16[2,128,128]{2,1,0:T(8,128)(2,1)S(1)}, bf16[2,128,128]{2,1,0:T(8,128)(2,1)S(1)}, u32[]{:S(2)}, u32[]{:S(2)}) collective-permute-start(bf16[2,128,128]{2,1,0:T(8,128)(2,1)S(1)} %get-tuple-element.32), channel_id=1, source_target_pairs={{0,28},{4,24},{8,20},{12,16},{16,12},{20,8},{24,4},{28,0},{1,29},{... | collective-permute-start | bytes 196616 | tf_op jit(solution)/shard_map/ppermute | solution.py:327
  30.5 4.0 %copy-start = (bf16[320,128,128]{2,1,0:T(8,128)(2,1)S(1)}, bf16[320,128,128]{2,1,0:T(8,128)(2,1)}, u32[]{:S(2)}) copy-start(bf16[320,128,128]{2,1,0:T(8,128)(2,1)} %tiles.1) | copy-start | bytes 31457284
  34.5 1.2 %copy-start.1 = (bf16[4096,128]{1,0:T(8,128)(2,1)S(1)}, bf16[4096,128]{1,0:T(8,128)(2,1)}, u32[]{:S(2)}) copy-start(bf16[4096,128]{1,0:T(8,128)(2,1)} %words.1) | copy-start | bytes 3145732
  35.7 0.7 copy-start.4
  41.0 0.7 %copy-start.3 = (s32[1,896]{1,0:T(1,128)S(1)}, s32[1,896]{1,0:T(1,128)}, u32[]{:S(2)}) copy-start(s32[1,896]{1,0:T(1,128)} %get-tuple-element.21.work) | copy-start | bytes 10756
  47.1 11.6 %all-to-all-start.1 = ((bf16[8,1,128,128]{3,2,1,0:T(8,128)(2,1)}), bf16[8,1,128,128]{3,2,1,0:T(8,128)(2,1)S(1)}, u32[]{:S(2)}, u32[]{:S(2)}) async-start(bf16[8,1,128,128]{3,2,1,0:T(8,128)(2,1)} %bitcast.4), calls=%async_computation.1 | async-start | bytes 524288 | tf_op jit(solution)/shard_map/all_to_all | solution.py:339
  59.5 1.9 %collective-permute-start.7 = (bf16[4,128,128]{2,1,0:T(8,128)(2,1)S(1)}, bf16[4,128,128]{2,1,0:T(8,128)(2,1)S(1)}, u32[]{:S(2)}, u32[]{:S(2)}) collective-permute-start(bf16[4,128,128]{2,1,0:T(8,128)(2,1)S(1)} %get-tuple-element.34), channel_id=1, source_target_pairs={{0,1},{1,0},{2,3},{3,2},{4,5},{5,4},{6,7},{7,6},{8,9},{9,8},{10,11... | collective-permute-start | bytes 393224 | tf_op jit(solution)/shard_map/ppermute | solution.py:346
  59.6 6.4 %collective-permute-start.8 = (bf16[4,128,128]{2,1,0:T(8,128)(2,1)S(1)}, bf16[4,128,128]{2,1,0:T(8,128)(2,1)S(1)}, u32[]{:S(2)}, u32[]{:S(2)}) collective-permute-start(bf16[4,128,128]{2,1,0:T(8,128)(2,1)S(1)} %get-tuple-element.35), channel_id=1, source_target_pairs={{0,2},{1,3},{2,0},{3,1},{4,6},{5,7},{6,4},{7,5},{8,10},{9,11},{10,... | collective-permute-start | bytes 393224 | tf_op jit(solution)/shard_map/ppermute | solution.py:346
  60.1 7.7 %collective-permute-start.9 = (bf16[4,128,128]{2,1,0:T(8,128)(2,1)S(1)}, bf16[4,128,128]{2,1,0:T(8,128)(2,1)S(1)}, u32[]{:S(2)}, u32[]{:S(2)}) collective-permute-start(bf16[4,128,128]{2,1,0:T(8,128)(2,1)S(1)} %get-tuple-element.36), channel_id=1, source_target_pairs={{0,3},{1,2},{2,1},{3,0},{4,7},{5,6},{6,5},{7,4},{8,11},{9,10},{10,... | collective-permute-start | bytes 393224 | tf_op jit(solution)/shard_map/ppermute | solution.py:346
where the time goes:
time: 69 us; the launch traced here: 68.5 us
  starting transfers between devices  23.8 us (34%)
  waiting for transfers between devices  20.3 us (29%)
  Pallas kernels  14.7 us (21%)
  local copies, waits for them, and re-layouts  8.26 us (12%)
  between operations  0.77 us (1%)
  other arithmetic  0.76 us (1%)
    ppermute x7, starting transfers between devices, body(): lax.ppermute(replies[d], 'wide', [(k, k ^ d) for k in range(wide)])  11.2 us
    unnamed x20, local copies, waits for them, and re-layouts  8.26 us
    all_to_all x1, waiting for transfers between devices, body(): lax.all_to_all(partial.reshape(wide, -1, side, width), 'wide', split_axis...  8.15 us
    all_to_all x1, starting transfers between devices, body(): lax.all_to_all(need, 'wide', split_axis=0, concat_axis=0, tiled=True)  7.28 us
    ppermute x3, waiting for transfers between devices, body(): lax.ppermute(pieces[d], 'narrow', [(n, n ^ d) for n in range(members)])  6.32 us
    all_to_all x1, waiting for transfers between devices, body(): lax.all_to_all(need, 'wide', split_axis=0, concat_axis=0, tiled=True)  5.77 us
    pallas_call x1, Pallas kernels, contract(): pl.pallas_call(contract_kernel, out_shape=jax.ShapeDtypeStruct((touched,...  5.43 us
    pallas_call x1, Pallas kernels, turn(): pl.pallas_call(functools.partial(turn_kernel, touched), out_shape=(jax.Sh...  4.53 us
  transfers between devices with their start and end apart: 12, of which 4 were waited for; matrix products, arithmetic and copies ran while one was open for 0% of the time, Pallas kernels for 9%

commit v1 on v0

--- a/solution.py
+++ b/solution.py
@@ -11,9 +11,9 @@
 ANSWER_MIB = 12
 RANK_MIB = 63
 TURN_MIB = 12
-TURN = 32
-GROUP = 4
-CHUNKS = 12
+TURN = 64
+GROUP = 2
+CHUNKS = 28
 SMEM = pl.BlockSpec(memory_space=pltpu.SMEM)
 VMEM = pl.BlockSpec(memory_space=pltpu.VMEM)
 HBM = pl.BlockSpec(memory_space=pltpu.HBM)

time: 69 us -> 68.6 us (level)
  no operation moved by 1% of the time
where the time goes in v1:
time: 68.6 us; the launch traced here: 68.2 us
  starting transfers between devices  23.8 us (35%)
  waiting for transfers between devices  20.3 us (30%)
  Pallas kernels  14.3 us (21%)
  local copies, waits for them, and re-layouts  8.26 us (12%)
  between operations  0.77 us (1%)
  other arithmetic  0.76 us (1%)
    ppermute x7, starting transfers between devices, body(): lax.ppermute(replies[d], 'wide', [(k, k ^ d) for k in range(wide)])  11.2 us
    unnamed x20, local copies, waits for them, and re-layouts  8.26 us
    all_to_all x1, waiting for transfers between devices, body(): lax.all_to_all(partial.reshape(wide, -1, side, width), 'wide', split_axis...  8.15 us
    all_to_all x1, starting transfers between devices, body(): lax.all_to_all(need, 'wide', split_axis=0, concat_axis=0, tiled=True)  7.28 us
    ppermute x3, waiting for transfers between devices, body(): lax.ppermute(pieces[d], 'narrow', [(n, n ^ d) for n in range(members)])  6.32 us
    all_to_all x1, waiting for transfers between devices, body(): lax.all_to_all(need, 'wide', split_axis=0, concat_axis=0, tiled=True)  5.77 us
    pallas_call x1, Pallas kernels, contract(): pl.pallas_call(contract_kernel, out_shape=jax.ShapeDtypeStruct((touched,...  5.35 us
    pallas_call x1, Pallas kernels, turn(): pl.pallas_call(functools.partial(turn_kernel, touched), out_shape=(jax.Sh...  4.22 us
  transfers between devices with their start and end apart: 12, of which 4 were waited for; matrix products, arithmetic and copies ran while one was open for 0% of the time, Pallas kernels for 9%

profile of v1, /device:TPU:0, one launch (start us, length us, event | category | flops | bytes accessed | tf_op | source)
XLA Modules:
  0.0 68.2 jit_solution(11055108299960111394)
XLA Ops:
  0.0 1.3 %ask.1 = s32[8,1,24]{2,1,0:T(1,128)} custom-call(s32[1,16]{1,0:T(1,128)} %user_need.1, s32[1,8]{1,0:T(1,128)} %item_need.1), custom_call_target="tpu_custom_call" | custom-call | tf_op jit(solution)/shard_map/ask/pallas_call | solution.py:176
  1.3 7.3 %all-to-all-start = ((s32[8,1,24]{2,1,0:T(1,128)}), s32[8,1,24]{2,1,0:T(1,128)S(1)}, u32[]{:S(2)}, u32[]{:S(2)}) async-start(s32[8,1,24]{2,1,0:T(1,128)} %ask.1), calls=%async_computation | async-start | bytes 8192 | tf_op jit(solution)/shard_map/all_to_all | solution.py:321
  9.3 5.8 %all-to-all-done.heard = s32[8,1,24]{2,1,0:T(1,128)S(1)} async-done(((s32[8,1,24]{2,1,0:T(1,128)}), s32[8,1,24]{2,1,0:T(1,128)S(1)}, u32[]{:S(2)}, u32[]{:S(2)}) %all-to-all-start) | async-done | bytes 800 | tf_op jit(solution)/shard_map/all_to_all | solution.py:321
  15.0 0.0 copy-start.8
  15.0 1.0 %copy-done.8 = bf16[2048,128]{1,0:T(8,128)(2,1)S(1)} copy-done((bf16[2048,128]{1,0:T(8,128)(2,1)S(1)}, bf16[2048,128]{1,0:T(8,128)(2,1)}, u32[]{:S(2)}) %copy-start.8) | copy-done | bytes 524312
  16.1 0.0 copy-start.9
  16.1 0.7 copy-done.9
  16.7 0.7 answer.1
  17.4 0.6 collective-permute-start
  18.0 0.0 copy-start.2
  18.0 0.0 copy-start.5
  18.0 0.6 collective-permute-start.1
  18.6 1.9 %rank.1 = (s32[1,640]{1,0:T(1,128)}, s32[1,1024]{1,0:T(1,128)}) custom-call(s32[1]{0:T(128)} %bitcast.me.owner, s32[1]{0:T(128)S(6)} %copy.15.live, s32[320]{0:T(512)} %user.1, s32[320]{0:T(512)} %item.1), custom_call_target="tpu_custom_call" | custom-call | flops 8589934592 | bytes 33554432 | tf_op jit(solution)/shard_map/rank/pallas_call | solution.py:89
  20.5 0.0 copy-start.7
  20.5 2.4 %collective-permute-start.2 = (bf16[2,128,128]{2,1,0:T(8,128)(2,1)S(1)}, bf16[2,128,128]{2,1,0:T(8,128)(2,1)S(1)}, u32[]{:S(2)}, u32[]{:S(2)}) collective-permute-start(bf16[2,128,128]{2,1,0:T(8,128)(2,1)S(1)} %get-tuple-element.28), channel_id=1, source_target_pairs={{0,12},{4,8},{8,4},{12,0},{16,28},{20,24},{24,20},{28,16},{1,13},{... | collective-permute-start | bytes 196616 | tf_op jit(solution)/shard_map/ppermute | solution.py:327
  22.8 0.6 collective-permute-start.3
  23.4 2.4 %collective-permute-start.4 = (bf16[2,128,128]{2,1,0:T(8,128)(2,1)S(1)}, bf16[2,128,128]{2,1,0:T(8,128)(2,1)S(1)}, u32[]{:S(2)}, u32[]{:S(2)}) collective-permute-start(bf16[2,128,128]{2,1,0:T(8,128)(2,1)S(1)} %get-tuple-element.30), channel_id=1, source_target_pairs={{0,20},{4,16},{8,28},{12,24},{16,4},{20,0},{24,12},{28,8},{1,21},{... | collective-permute-start | bytes 196616 | tf_op jit(solution)/shard_map/ppermute | solution.py:327
  25.7 0.0 collective-permute-done.refs_1_
  25.8 0.6 collective-permute-start.5
  26.3 0.0 collective-permute-done.1.refs_2_
  26.3 4.1 %collective-permute-start.6 = (bf16[2,128,128]{2,1,0:T(8,128)(2,1)S(1)}, bf16[2,128,128]{2,1,0:T(8,128)(2,1)S(1)}, u32[]{:S(2)}, u32[]{:S(2)}) collective-permute-start(bf16[2,128,128]{2,1,0:T(8,128)(2,1)S(1)} %get-tuple-element.32), channel_id=1, source_target_pairs={{0,28},{4,24},{8,20},{12,16},{16,12},{20,8},{24,4},{28,0},{1,29},{... | collective-permute-start | bytes 196616 | tf_op jit(solution)/shard_map/ppermute | solution.py:327
  30.5 0.0 copy-done.2
  30.5 0.0 copy-done.5
  30.5 0.0 copy-done.6
  30.5 0.0 copy-start
  30.5 4.0 %copy-done = bf16[320,128,128]{2,1,0:T(8,128)(2,1)S(1)} copy-done((bf16[320,128,128]{2,1,0:T(8,128)(2,1)S(1)}, bf16[320,128,128]{2,1,0:T(8,128)(2,1)}, u32[]{:S(2)}) %copy-start) | copy-done | bytes 10485784
  34.5 1.2 %copy-done.1 = bf16[4096,128]{1,0:T(8,128)(2,1)S(1)} copy-done((bf16[4096,128]{1,0:T(8,128)(2,1)S(1)}, bf16[4096,128]{1,0:T(8,128)(2,1)}, u32[]{:S(2)}) %copy-start.1) | copy-done | bytes 1048600
  35.7 0.7 copy-done.4
  36.4 4.2 %turn.1 = (bf16[408,128,128]{2,1,0:T(8,128)(2,1)S(1)}, f32[408,128]{1,0:T(8,128)S(1)}) custom-call(s32[1,640]{1,0:T(1,128)S(1)} %copy-done.4, s32[320]{0:T(512)S(1)} %copy-done.5, s32[320]{0:T(512)S(1)} %copy-done.6, bf16[320,128,128]{2,1,0:T(8,128)(2,1)S(1)} %copy-done, bf16[4096,128]{1,0:T(8,128)(2,1)S(1)} %copy-done.1, bf16[1000,128]{1,0:T(8,128)(2,1)S(1)} %copy-done.2), custom_call_target="tpu_custom_call" | custom-call | flops 1073741824 | bytes 20971520 | tf_op jit(solution)/shard_map/turn/pallas_call | solution.py:147
  40.6 0.0 collective-permute-done.2.refs_3_
  40.6 0.0 collective-permute-done.3.refs_4_
  40.6 0.0 collective-permute-done.4.refs_5_
  40.6 0.0 collective-permute-done.5.refs_6_
  40.6 0.0 collective-permute-done.6.refs_7_
  40.7 0.0 copy-start.3
  40.7 0.7 copy-done.3
  41.3 5.3 %contract.1 = bf16[8,128,128]{2,1,0:T(8,128)(2,1)} custom-call(s32[1,1024]{1,0:T(1,128)S(1)} %copy-done.3, f32[408,128]{1,0:T(8,128)S(1)} %get-tuple-element.23.scale, bf16[408,128,128]{2,1,0:T(8,128)(2,1)S(1)} %get-tuple-element.24.turned, bf16[2,128,128]{2,1,0:T(8,128)(2,1)S(1)} %get-tuple-element.25.refs_0_, ...), custom_call_target="tpu_custom_call" | custom-call | flops 1711276032 | bytes 6684672 | tf_op jit(solution)/shard_map/contract/pallas_call | solution.py:243
  46.7 3.4 %all-to-all-start.1 = ((bf16[8,1,128,128]{3,2,1,0:T(8,128)(2,1)}), bf16[8,1,128,128]{3,2,1,0:T(8,128)(2,1)S(1)}, u32[]{:S(2)}, u32[]{:S(2)}) async-start(bf16[8,1,128,128]{3,2,1,0:T(8,128)(2,1)} %bitcast.4), calls=%async_computation.1 | async-start | bytes 524288 | tf_op jit(solution)/shard_map/all_to_all | solution.py:339
  50.1 8.2 %all-to-all-done.1 = bf16[8,1,128,128]{3,2,1,0:T(8,128)(2,1)S(1)} async-done(((bf16[8,1,128,128]{3,2,1,0:T(8,128)(2,1)}), bf16[8,1,128,128]{3,2,1,0:T(8,128)(2,1)S(1)}, u32[]{:S(2)}, u32[]{:S(2)}) %all-to-all-start.1) | async-done | bytes 262176 | tf_op jit(solution)/shard_map/all_to_all | solution.py:339
  58.3 0.0 copy-done.7
  58.3 0.9 %merge.1 = (f32[4,128,128]{2,1,0:T(8,128)S(1)}, bf16[4,128,128]{2,1,0:T(8,128)(2,1)S(1)}, bf16[4,128,128]{2,1,0:T(8,128)(2,1)S(1)}, bf16[4,128,128]{2,1,0:T(8,128)(2,1)S(1)}) custom-call(s32[1]{0:T(128)} %bitcast.me.owner, s32[1]{0:T(128)} %bitcast.1.me, s32[8,1,24]{2,1,0:T(1,128)S(1)} %all-to-all-done.heard, s32[128]{0:T(128)S(1)} %copy-done.7, ...), custom_call_target="tpu_custom_call" | custom-call | tf_op jit(solution)/shard_map/merge/pallas_call | solution.py:287
  59.1 0.1 collective-permute-start.7
  59.2 0.9 %collective-permute-start.8 = (bf16[4,128,128]{2,1,0:T(8,128)(2,1)S(1)}, bf16[4,128,128]{2,1,0:T(8,128)(2,1)S(1)}, u32[]{:S(2)}, u32[]{:S(2)}) collective-permute-start(bf16[4,128,128]{2,1,0:T(8,128)(2,1)S(1)} %get-tuple-element.35), channel_id=1, source_target_pairs={{0,2},{1,3},{2,0},{3,1},{4,6},{5,7},{6,4},{7,5},{8,10},{9,11},{10,... | collective-permute-start | bytes 393224 | tf_op jit(solution)/shard_map/ppermute | solution.py:346
  60.2 0.9 %collective-permute-start.9 = (bf16[4,128,128]{2,1,0:T(8,128)(2,1)S(1)}, bf16[4,128,128]{2,1,0:T(8,128)(2,1)S(1)}, u32[]{:S(2)}, u32[]{:S(2)}) collective-permute-start(bf16[4,128,128]{2,1,0:T(8,128)(2,1)S(1)} %get-tuple-element.36), channel_id=1, source_target_pairs={{0,3},{1,2},{2,1},{3,0},{4,7},{5,6},{6,5},{7,4},{8,11},{9,10},{10,... | collective-permute-start | bytes 393224 | tf_op jit(solution)/shard_map/ppermute | solution.py:346
  61.1 0.0 collective-permute-done.7
  61.1 4.6 %collective-permute-done.8 = bf16[4,128,128]{2,1,0:T(8,128)(2,1)S(1)} collective-permute-done((bf16[4,128,128]{2,1,0:T(8,128)(2,1)S(1)}, bf16[4,128,128]{2,1,0:T(8,128)(2,1)S(1)}, u32[]{:S(2)}, u32[]{:S(2)}) %collective-permute-start.8) | collective-permute-done | bytes 131104 | tf_op jit(solution)/shard_map/ppermute | solution.py:346
  65.7 1.7 %collective-permute-done.9 = bf16[4,128,128]{2,1,0:T(8,128)(2,1)S(1)} collective-permute-done((bf16[4,128,128]{2,1,0:T(8,128)(2,1)S(1)}, bf16[4,128,128]{2,1,0:T(8,128)(2,1)S(1)}, u32[]{:S(2)}, u32[]{:S(2)}) %collective-permute-start.9) | collective-permute-done | bytes 131104 | tf_op jit(solution)/shard_map/ppermute | solution.py:346
  67.4 0.8 %convert_add_fusion = f32[4,128,128]{2,1,0:T(8,128)} fusion(bf16[4,128,128]{2,1,0:T(8,128)(2,1)S(1)} %collective-permute-done.9, bf16[4,128,128]{2,1,0:T(8,128)(2,1)S(1)} %collective-permute-done.8, f32[4,128,128]{2,1,0:T(8,128)S(1)} %get-tuple-element.33, bf16[4,128,128]{2,1,0:T(8,128)(2,1)S(1)} %collective-permute-done.7), kind=kLoop, calls=%fused_computation | loop fusion | flops 393216 | bytes 917504 | tf_op jit(solution)/shard_map/add | solution.py:347
  (3 shorter events, 0.0 us)
Async XLA Ops:
  1.3 13.7 %all-to-all-start = ((s32[8,1,24]{2,1,0:T(1,128)}), s32[8,1,24]{2,1,0:T(1,128)S(1)}, u32[]{:S(2)}, u32[]{:S(2)}) async-start(s32[8,1,24]{2,1,0:T(1,128)} %ask.1), calls=%async_computation | async-start | bytes 8192 | tf_op jit(solution)/shard_map/all_to_all | solution.py:321
  15.0 1.0 %copy-start.8 = (bf16[2048,128]{1,0:T(8,128)(2,1)S(1)}, bf16[2048,128]{1,0:T(8,128)(2,1)}, u32[]{:S(2)}) copy-start(bf16[2048,128]{1,0:T(8,128)(2,1)} %param.23) | copy-start | bytes 1572868
  16.1 0.7 copy-start.9
  17.4 8.3 %collective-permute-start = (bf16[2,128,128]{2,1,0:T(8,128)(2,1)S(1)}, bf16[2,128,128]{2,1,0:T(8,128)(2,1)S(1)}, u32[]{:S(2)}, u32[]{:S(2)}) collective-permute-start(bf16[2,128,128]{2,1,0:T(8,128)(2,1)S(1)} %get-tuple-element.26), channel_id=1, source_target_pairs={{0,4},{4,0},{8,12},{12,8},{16,20},{20,16},{24,28},{28,24},{1,5},{5... | collective-permute-start | bytes 196616 | tf_op jit(solution)/shard_map/ppermute | solution.py:327
  18.0 12.5 %copy-start.2 = (bf16[1000,128]{1,0:T(8,128)(2,1)S(1)}, bf16[1000,128]{1,0:T(8,128)(2,1)}, u32[]{:S(2)}) copy-start(bf16[1000,128]{1,0:T(8,128)(2,1)} %months.1) | copy-start | bytes 768004
  18.0 12.5 %copy-start.5 = (s32[320]{0:T(512)S(1)}, s32[320]{0:T(512)}, u32[]{:S(2)}) copy-start(s32[320]{0:T(512)} %word.1) | copy-start | bytes 3844
  18.0 12.5 %copy-start.6 = (s32[320]{0:T(512)S(1)}, s32[320]{0:T(512)}, u32[]{:S(2)}) copy-start(s32[320]{0:T(512)} %month.1) | copy-start | bytes 3844
  18.0 8.3 %collective-permute-start.1 = (bf16[2,128,128]{2,1,0:T(8,128)(2,1)S(1)}, bf16[2,128,128]{2,1,0:T(8,128)(2,1)S(1)}, u32[]{:S(2)}, u32[]{:S(2)}) collective-permute-start(bf16[2,128,128]{2,1,0:T(8,128)(2,1)S(1)} %get-tuple-element.27), channel_id=1, source_target_pairs={{0,8},{4,12},{8,0},{12,4},{16,24},{20,28},{24,16},{28,20},{1,9},{5... | collective-permute-start | bytes 196616 | tf_op jit(solution)/shard_map/ppermute | solution.py:327
  20.5 37.8 %copy-start.7 = (s32[128]{0:T(128)S(1)}, s32[128]{0:T(128)}, u32[]{:S(2)}) copy-start(s32[128]{0:T(128)} %slot.3) | copy-start | bytes 1540
  20.5 20.1 %collective-permute-start.2 = (bf16[2,128,128]{2,1,0:T(8,128)(2,1)S(1)}, bf16[2,128,128]{2,1,0:T(8,128)(2,1)S(1)}, u32[]{:S(2)}, u32[]{:S(2)}) collective-permute-start(bf16[2,128,128]{2,1,0:T(8,128)(2,1)S(1)} %get-tuple-element.28), channel_id=1, source_target_pairs={{0,12},{4,8},{8,4},{12,0},{16,28},{20,24},{24,20},{28,16},{1,13},{... | collective-permute-start | bytes 196616 | tf_op jit(solution)/shard_map/ppermute | solution.py:327
  22.8 17.8 %collective-permute-start.3 = (bf16[2,128,128]{2,1,0:T(8,128)(2,1)S(1)}, bf16[2,128,128]{2,1,0:T(8,128)(2,1)S(1)}, u32[]{:S(2)}, u32[]{:S(2)}) collective-permute-start(bf16[2,128,128]{2,1,0:T(8,128)(2,1)S(1)} %get-tuple-element.29), channel_id=1, source_target_pairs={{0,16},{4,20},{8,24},{12,28},{16,0},{20,4},{24,8},{28,12},{1,17},{... | collective-permute-start | bytes 196616 | tf_op jit(solution)/shard_map/ppermute | solution.py:327
  23.4 17.2 %collective-permute-start.4 = (bf16[2,128,128]{2,1,0:T(8,128)(2,1)S(1)}, bf16[2,128,128]{2,1,0:T(8,128)(2,1)S(1)}, u32[]{:S(2)}, u32[]{:S(2)}) collective-permute-start(bf16[2,128,128]{2,1,0:T(8,128)(2,1)S(1)} %get-tuple-element.30), channel_id=1, source_target_pairs={{0,20},{4,16},{8,28},{12,24},{16,4},{20,0},{24,12},{28,8},{1,21},{... | collective-permute-start | bytes 196616 | tf_op jit(solution)/shard_map/ppermute | solution.py:327
  25.8 14.9 %collective-permute-start.5 = (bf16[2,128,128]{2,1,0:T(8,128)(2,1)S(1)}, bf16[2,128,128]{2,1,0:T(8,128)(2,1)S(1)}, u32[]{:S(2)}, u32[]{:S(2)}) collective-permute-start(bf16[2,128,128]{2,1,0:T(8,128)(2,1)S(1)} %get-tuple-element.31), channel_id=1, source_target_pairs={{0,24},{4,28},{8,16},{12,20},{16,8},{20,12},{24,0},{28,4},{1,25},{... | collective-permute-start | bytes 196616 | tf_op jit(solution)/shard_map/ppermute | solution.py:327
  26.3 14.3 %collective-permute-start.6 = (bf16[2,128,128]{2,1,0:T(8,128)(2,1)S(1)}, bf16[2,128,128]{2,1,0:T(8,128)(2,1)S(1)}, u32[]{:S(2)}, u32[]{:S(2)}) collective-permute-start(bf16[2,128,128]{2,1,0:T(8,128)(2,1)S(1)} %get-tuple-element.32), channel_id=1, source_target_pairs={{0,28},{4,24},{8,20},{12,16},{16,12},{20,8},{24,4},{28,0},{1,29},{... | collective-permute-start | bytes 196616 | tf_op jit(solution)/shard_map/ppermute | solution.py:327
  30.5 4.0 %copy-start = (bf16[320,128,128]{2,1,0:T(8,128)(2,1)S(1)}, bf16[320,128,128]{2,1,0:T(8,128)(2,1)}, u32[]{:S(2)}) copy-start(bf16[320,128,128]{2,1,0:T(8,128)(2,1)} %tiles.1) | copy-start | bytes 31457284
  34.5 1.2 %copy-start.1 = (bf16[4096,128]{1,0:T(8,128)(2,1)S(1)}, bf16[4096,128]{1,0:T(8,128)(2,1)}, u32[]{:S(2)}) copy-start(bf16[4096,128]{1,0:T(8,128)(2,1)} %words.1) | copy-start | bytes 3145732
  35.7 0.7 copy-start.4
  40.7 0.7 %copy-start.3 = (s32[1,1024]{1,0:T(1,128)S(1)}, s32[1,1024]{1,0:T(1,128)}, u32[]{:S(2)}) copy-start(s32[1,1024]{1,0:T(1,128)} %get-tuple-element.21.work) | copy-start | bytes 12292
  46.7 11.6 %all-to-all-start.1 = ((bf16[8,1,128,128]{3,2,1,0:T(8,128)(2,1)}), bf16[8,1,128,128]{3,2,1,0:T(8,128)(2,1)S(1)}, u32[]{:S(2)}, u32[]{:S(2)}) async-start(bf16[8,1,128,128]{3,2,1,0:T(8,128)(2,1)} %bitcast.4), calls=%async_computation.1 | async-start | bytes 524288 | tf_op jit(solution)/shard_map/all_to_all | solution.py:339
  59.1 1.9 %collective-permute-start.7 = (bf16[4,128,128]{2,1,0:T(8,128)(2,1)S(1)}, bf16[4,128,128]{2,1,0:T(8,128)(2,1)S(1)}, u32[]{:S(2)}, u32[]{:S(2)}) collective-permute-start(bf16[4,128,128]{2,1,0:T(8,128)(2,1)S(1)} %get-tuple-element.34), channel_id=1, source_target_pairs={{0,1},{1,0},{2,3},{3,2},{4,5},{5,4},{6,7},{7,6},{8,9},{9,8},{10,11... | collective-permute-start | bytes 393224 | tf_op jit(solution)/shard_map/ppermute | solution.py:346
  59.2 6.4 %collective-permute-start.8 = (bf16[4,128,128]{2,1,0:T(8,128)(2,1)S(1)}, bf16[4,128,128]{2,1,0:T(8,128)(2,1)S(1)}, u32[]{:S(2)}, u32[]{:S(2)}) collective-permute-start(bf16[4,128,128]{2,1,0:T(8,128)(2,1)S(1)} %get-tuple-element.35), channel_id=1, source_target_pairs={{0,2},{1,3},{2,0},{3,1},{4,6},{5,7},{6,4},{7,5},{8,10},{9,11},{10,... | collective-permute-start | bytes 393224 | tf_op jit(solution)/shard_map/ppermute | solution.py:346
  60.2 7.2 %collective-permute-start.9 = (bf16[4,128,128]{2,1,0:T(8,128)(2,1)S(1)}, bf16[4,128,128]{2,1,0:T(8,128)(2,1)S(1)}, u32[]{:S(2)}, u32[]{:S(2)}) collective-permute-start(bf16[4,128,128]{2,1,0:T(8,128)(2,1)S(1)} %get-tuple-element.36), channel_id=1, source_target_pairs={{0,3},{1,2},{2,1},{3,0},{4,7},{5,6},{6,5},{7,4},{8,11},{9,10},{10,... | collective-permute-start | bytes 393224 | tf_op jit(solution)/shard_map/ppermute | solution.py:346
